TPU v7x, 32 devices: a whole 2x2x4 slice. The times are simulated.
32 devices in a mesh: rows: 16 (over z, y, x), rep: 2 (over core).
Axes of the slice: x: 2, y: 2, z: 4, core: 2. Of those that a mesh axis runs over, the one named last changes fastest.
Arguments:
- grad_out: bfloat16 [2048, 1024], P('rows'), may hold values from -8 to 8
- w_self: bfloat16 [1024, 1024], replicated, may hold values from -0.1875 to 0.1875
- w_neigh: bfloat16 [1024, 1024], replicated, may hold values from -0.1875 to 0.1875
- adj_tiles: bfloat16 [16, 8, 128, 128], P('rows'), may hold values from -0.3125 to 0.3125
- tile_index: int32 [16, 8], P('rows'), may hold values from 0 to 15, as said below
- tile_count: int32 [16], P('rows'), may hold values from 4 to 8, as said below
- prompt_ids: int32 [2048], P('rows'), may hold values from 0 to 15
Outputs:
- input_grad: bfloat16 [2048, 1024], P('rows')
- prompt_grad: float32 [16, 1024], replicated
Inputs may be any that keep to these rules, and one draw needn't show every extreme that they name: `tile_index`: each row holds 8 different tile numbers; only the first tile_count entries of a row are used. `tile_count`: some destination tile uses all 8 slots.
All inputs are finite; a program needn't handle non-finite values.
Results may differ from a plain program's by a relative error of at most 0.0041.
Values may be sent and summed in bfloat16 or wider, within the bound.
A program may use at most 64 MiB of HBM per device.

v0:
```python
import math
import jax
import jax.numpy as jnp
from jax import lax
from jax.sharding import PartitionSpec as P

PROMPTS = 16


def shards(grad_out, w_self, w_neigh, adj_tiles, tile_index, tile_count, prompt_ids):
    rows_dev, width = grad_out.shape
    local_tiles, max_slots, tile_size, _ = adj_tiles.shape
    n_rows = lax.axis_size("rows")
    n_rep = lax.axis_size("rep")
    rep_index = lax.axis_index("rep")
    total_tiles = local_tiles * n_rows
    slot_ids = jnp.arange(max_slots)
    in_use = slot_ids[None, :] < tile_count[:, None]
    matches = (tile_index[:, :, None] == jnp.arange(total_tiles)[None, None, :]) & in_use[
        :, :, None
    ]
    present = jnp.any(matches, axis=1)
    slot_table = jnp.argmax(matches, axis=1)
    contract = (((1,), (1,)), ((), ()))
    half_rows = rows_dev // n_rep
    mine = lax.dynamic_slice_in_dim(grad_out, rep_index * half_rows, half_rows, 0)
    initial = jnp.zeros((local_tiles, tile_size, width), jnp.float32)

    def half_column(place):
        return place // half_rows * rows_dev + rep_index * half_rows + place % half_rows

    piece = lax.all_gather(mine, "rows", axis=0, tiled=True)
    piece_rows = piece.shape[0]
    unit = math.gcd(math.gcd(piece_rows, tile_size), half_rows)
    segments = piece_rows // unit
    feat = piece.shape[1]

    def one_segment(index, carry):
        start = index * unit
        rows_part = lax.dynamic_slice_in_dim(piece, start, unit, 0)
        column = half_column(start)
        source = column // tile_size
        offset = column % tile_size
        slot = slot_table[0, source]
        zero = jnp.zeros((), jnp.int32)
        block = lax.dynamic_slice(
            adj_tiles, (jnp.int32(0), slot, zero, offset), (1, 1, tile_size, unit)
        )
        block = block.reshape(tile_size, unit)

        def product(args):
            blk, part_rows = args
            return jnp.dot(blk, part_rows, preferred_element_type=jnp.float32)

        def nothing(args):
            return jnp.zeros((tile_size, feat), jnp.float32)

        term = lax.cond(present[0, source], product, nothing, (block, rows_part))
        updated = [carry[0] + term]
        return jnp.stack(updated, axis=0)

    partial_value = lax.fori_loop(0, segments, one_segment, initial)
    summed = lax.psum(partial_value.reshape(rows_dev, width), "rep")
    aggregate = summed.astype(jnp.bfloat16)
    full_grad = lax.dot_general(grad_out, w_self, contract, preferred_element_type=jnp.float32)
    full_grad = full_grad + lax.dot_general(
        aggregate, w_neigh, contract, preferred_element_type=jnp.float32
    )
    onehot = (prompt_ids[None, :] == jnp.arange(PROMPTS)[:, None]).astype(jnp.float32)
    prompt_part = jnp.dot(onehot, full_grad, precision=lax.Precision.HIGHEST)
    prompt_grad = lax.psum(prompt_part, "rows")
    return (full_grad.astype(jnp.bfloat16), prompt_grad)


def solution(mesh):
    placed = (
        P("rows", None),
        P(),
        P(),
        P("rows", None, None, None),
        P("rows", None),
        P("rows"),
        P("rows"),
    )
    return jax.shard_map(
        shards, mesh=mesh, in_specs=placed, out_specs=(P("rows", None), P()), check_vma=False
    )
```

profile of v0, /device:TPU:0, one launch (start us, length us, event | category | flops | bytes accessed | tf_op | source)
XLA Modules:
  0.0 249.7 jit_solution(9167569189331557641)
XLA Ops:
  7.2 1.7 constant_dynamic-slice_fusion.2
  10.4 1.3 iota_reduce_fusion
  11.7 3.3 %fusion.13 = f32[128,1024]{1,0:T(8,128)} fusion(bf16[128,1024]{1,0:T(8,128)(2,1)} %param.11, bf16[1024,1024]{1,0:T(8,128)(2,1)} %param.12), kind=kOutput, calls=%fused_computation.22 | convolution fusion | flops 268435456 | bytes 2883584 | tf_op jit(solution)/shard_map/dot_general | solution.py:65
  15.0 59.5 %all-gather.2.cloned.1.call-done = bf16[1024,1024]{1,0:T(8,128)(2,1)} async-done(((bf16[64,1024]{1,0:T(8,128)(2,1)}), bf16[1024,1024]{1,0:T(8,128)(2,1)}) %all-gather.2.cloned.1.call-update) | async-done | bytes 2097168 | tf_op jit(solution)/shard_map/all_gather | solution.py:32
  74.5 45.9 %while.16 = (s32[]{:T(128)}, f32[1,128,1024]{2,1,0:T(8,128)S(1)}, s32[]{:T(128)}, pred[1,16]{1,0:T(4,128)(4,1)S(1)}, s32[1,16]{1,0:T(1,128)S(1)}, /*index=5*/bf1...) while((s32[]{:T(128)}, f32[1,128,1024]{2,1,0:T(8,128)S(1)}, ...), condition=%wide.region_5.6_spmd, body=%wide.region_2.5_spmd.sunk | while | flops 16908344 | bytes 2261804 | solution.py:62
  75.3 4.7 %conditional.2 = (f32[128,1024]{1,0:T(8,128)S(1)}) conditional(s32[]{:T(128)} %bitcast.25, () %tuple.66, (s32[1,16]{1,0:T(1,128)S(1)}, s32[]{:T(128)}, s32[]{:T(128)}, bf16[1,8,128,128]{3,2,1,0:T(8,128)(2,1)}, s32[]{:T(128)}, /*index=5*/pred[]{:T(512)}, bf16[1024,1024]{1,0:T(8,128)(2,1)}) %tuple.67), branch_computations={%region_3.3_spmd, %region_4.4_spmd} | conditional | flops 16777228 | bytes 688299 | solution.py:58
  78.7 1.2 fusion
  80.8 4.7 %conditional.2 = (f32[128,1024]{1,0:T(8,128)S(1)}) conditional(s32[]{:T(128)} %bitcast.25, () %tuple.66, (s32[1,16]{1,0:T(1,128)S(1)}, s32[]{:T(128)}, s32[]{:T(128)}, bf16[1,8,128,128]{3,2,1,0:T(8,128)(2,1)}, s32[]{:T(128)}, /*index=5*/pred[]{:T(512)}, bf16[1024,1024]{1,0:T(8,128)(2,1)}) %tuple.67), branch_computations={%region_3.3_spmd, %region_4.4_spmd} | conditional | flops 16777228 | bytes 688299 | solution.py:58
  84.3 1.2 fusion
  86.4 0.8 conditional.2
  88.0 0.8 conditional.2
  89.7 0.8 conditional.2
  91.3 4.7 %conditional.2 = (f32[128,1024]{1,0:T(8,128)S(1)}) conditional(s32[]{:T(128)} %bitcast.25, () %tuple.66, (s32[1,16]{1,0:T(1,128)S(1)}, s32[]{:T(128)}, s32[]{:T(128)}, bf16[1,8,128,128]{3,2,1,0:T(8,128)(2,1)}, s32[]{:T(128)}, /*index=5*/pred[]{:T(512)}, bf16[1024,1024]{1,0:T(8,128)(2,1)}) %tuple.67), branch_computations={%region_3.3_spmd, %region_4.4_spmd} | conditional | flops 16777228 | bytes 688299 | solution.py:58
  94.8 1.2 fusion
  96.9 4.7 %conditional.2 = (f32[128,1024]{1,0:T(8,128)S(1)}) conditional(s32[]{:T(128)} %bitcast.25, () %tuple.66, (s32[1,16]{1,0:T(1,128)S(1)}, s32[]{:T(128)}, s32[]{:T(128)}, bf16[1,8,128,128]{3,2,1,0:T(8,128)(2,1)}, s32[]{:T(128)}, /*index=5*/pred[]{:T(512)}, bf16[1024,1024]{1,0:T(8,128)(2,1)}) %tuple.67), branch_computations={%region_3.3_spmd, %region_4.4_spmd} | conditional | flops 16777228 | bytes 688299 | solution.py:58
  100.3 1.2 fusion
  107.3 4.7 %conditional.2 = (f32[128,1024]{1,0:T(8,128)S(1)}) conditional(s32[]{:T(128)} %bitcast.25, () %tuple.66, (s32[1,16]{1,0:T(1,128)S(1)}, s32[]{:T(128)}, s32[]{:T(128)}, bf16[1,8,128,128]{3,2,1,0:T(8,128)(2,1)}, s32[]{:T(128)}, /*index=5*/pred[]{:T(512)}, bf16[1024,1024]{1,0:T(8,128)(2,1)}) %tuple.67), branch_computations={%region_3.3_spmd, %region_4.4_spmd} | conditional | flops 16777228 | bytes 688299 | solution.py:58
  110.8 1.2 fusion
  112.9 0.8 conditional.2
  120.4 4.8 %all-reduce.4 = bf16[128,1024]{1,0:T(8,128)(2,1)S(1)} all-reduce(f32[128,1024]{1,0:T(8,128)S(1)} %bitcast.27), channel_id=1, replica_groups=mesh['rows'=16,'rep'=2] {'rep'}, use_global_device_ids=true, to_apply=%region_6.7 | all-reduce | flops 131072 | bytes 786432 | tf_op jit(solution)/shard_map/psum | solution.py:63
  125.2 2.6 %fusion.12 = (bf16[128,1024]{1,0:T(8,128)(2,1)}, f32[128,1024]{1,0:T(8,128)S(1)}) fusion(f32[128,1024]{1,0:T(8,128)} %fusion.13, bf16[128,1024]{1,0:T(8,128)(2,1)S(1)} %all-reduce.4, bf16[1024,1024]{1,0:T(8,128)(2,1)S(1)} %copy-done), kind=kOutput, calls=%fused_computation.21 | convolution fusion | flops 268697600 | bytes 3670016 | tf_op jit(solution)/shard_map/dot_general | solution.py:66
  127.8 0.9 fusion.7
  128.8 112.6 %all-reduce.3.cloned.1.call-done = f32[16,1024]{1,0:T(8,128)} async-done(((f32[16,1024]{1,0:T(8,128)}), f32[16,1024]{1,0:T(8,128)}) %all-reduce.3.cloned.1.call-update) | async-done | bytes 65552 | tf_op jit(solution)/shard_map/psum | solution.py:71
  241.4 1.5 copy.21
  (66 shorter events, 22.8 us)
Async XLA Ops:
  7.2 118.1 %copy-start = (bf16[1024,1024]{1,0:T(8,128)(2,1)S(1)}, bf16[1024,1024]{1,0:T(8,128)(2,1)}, u32[]{:S(2)}) copy-start(bf16[1024,1024]{1,0:T(8,128)(2,1)} %param.13) | copy-start | bytes 6291460
  7.2 67.3 %all-gather.2.cloned.1.call-start = ((), (), s32[]{:S(2)}) async-start(), calls=%async_computation | async-start | bytes 2228224 | tf_op jit(solution)/shard_map/all_gather | solution.py:32
  9.0 232.4 %all-reduce.3.cloned.1.call-start = ((), (), s32[]{:S(2)}) async-start(), calls=%async_computation.1 | async-start | bytes 131072 | tf_op jit(solution)/shard_map/psum | solution.py:71
  120.4 7.4 %copy-start.1 = (s32[128]{0:T(128)S(1)}, s32[128]{0:T(128)}, u32[]{:S(2)}) copy-start(s32[128]{0:T(128)} %param.17) | copy-start | bytes 1540
Sparse Core Ops, SparseCore 0:
  11.3 63.0 all-gather.1
  128.9 112.4 all-reduce.2
where the time goes:
time: 250 us
  waiting for transfers between devices  172 us (69%)
  loops' own time  23.3 us (9%)
  other arithmetic  14.8 us (6%)
  between operations  14.7 us (6%)
  matrix products  12.8 us (5%)
  local copies, waits for them, and re-layouts  7.06 us (3%)
  blocking collectives  4.82 us (2%)
    psum x1, waiting for transfers between devices, shards(): prompt_grad = lax.psum(prompt_part, 'rows')  113 us
    all_gather x1, waiting for transfers between devices, shards(): piece = lax.all_gather(mine, 'rows', axis=0, tiled=True)  59.5 us
    another operation x16, loops' own time, one_segment(): term = lax.cond(present[0, source], product, nothing, (block, rows_part))  21.9 us
    convert_element_type x16, other arithmetic, one_segment(): term = lax.cond(present[0, source], product, nothing, (block, rows_part))  10.6 us
    dot_general x5, matrix products, product(): return jnp.dot(blk, part_rows, preferred_element_type=jnp.float32)  5.96 us
  transfers between devices with their start and end apart: 2, of which 2 were waited for; matrix products, arithmetic and copies ran while one was open for 2% of the time, Pallas kernels for 0%

commit v1 on v0

--- a/solution.py
+++ b/solution.py
@@ -68,7 +68,7 @@
     )
     onehot = (prompt_ids[None, :] == jnp.arange(PROMPTS)[:, None]).astype(jnp.float32)
     prompt_part = jnp.dot(onehot, full_grad, precision=lax.Precision.HIGHEST)
-    prompt_grad = lax.psum(prompt_part, "rows")
+    prompt_grad = jnp.sum(lax.all_gather(prompt_part, axis_name="rows"), axis=0)
     return (full_grad.astype(jnp.bfloat16), prompt_grad)
 
 

time: 250 us -> 203 us (0.81)
  waiting for transfers between devices: 172 us -> 124 us
    psum x1 -> x0, waiting for transfers between devices: 113 us -> none  [shards(): prompt_grad = lax.psum(prompt_part, 'rows')]
    all_gather x0 -> x1, waiting for transfers between devices: none -> 64.2 us  [shards(): prompt_grad = jnp.sum(lax.all_gather(prompt_part, axis_name='rows'), axis=0)]
  transfers between devices with their start and end apart: 2 -> 2, of which waited for: 2 -> 2; matrix products, arithmetic and copies ran while one was open for 2% -> 3% of each run, Pallas kernels for 0% -> 0%
where the time goes in v1:
time: 203 us; the launch traced here: 202 us
  waiting for transfers between devices  124 us (61%)
  loops' own time  23.3 us (11%)
  other arithmetic  16.7 us (8%)
  between operations  14.7 us (7%)
  matrix products  12.8 us (6%)
  local copies, waits for them, and re-layouts  5.59 us (3%)
  blocking collectives  4.82 us (2%)
    all_gather x1, waiting for transfers between devices, shards(): prompt_grad = jnp.sum(lax.all_gather(prompt_part, axis_name='rows'), axis=0)  64.2 us
    all_gather x1, waiting for transfers between devices, shards(): piece = lax.all_gather(mine, 'rows', axis=0, tiled=True)  59.5 us
    another operation x16, loops' own time, one_segment(): term = lax.cond(present[0, source], product, nothing, (block, rows_part))  21.9 us
    convert_element_type x16, other arithmetic, one_segment(): term = lax.cond(present[0, source], product, nothing, (block, rows_part))  10.6 us
    dot_general x5, matrix products, product(): return jnp.dot(blk, part_rows, preferred_element_type=jnp.float32)  5.96 us
    psum x1, blocking collectives, shards(): summed = lax.psum(partial_value.reshape(rows_dev, width), 'rep')  4.82 us
  transfers between devices with their start and end apart: 2, of which 2 were waited for; matrix products, arithmetic and copies ran while one was open for 3% of the time, Pallas kernels for 0%

profile of v1, /device:TPU:0, one launch (start us, length us, event | category | flops | bytes accessed | tf_op | source)
XLA Modules:
  0.0 201.8 jit_solution(6527669584327510367)
XLA Ops:
  7.2 1.7 constant_dynamic-slice_fusion.2
  10.4 1.3 iota_reduce_fusion
  11.7 3.3 %fusion.13 = f32[128,1024]{1,0:T(8,128)} fusion(bf16[128,1024]{1,0:T(8,128)(2,1)} %param.11, bf16[1024,1024]{1,0:T(8,128)(2,1)} %param.12), kind=kOutput, calls=%fused_computation.22 | convolution fusion | flops 268435456 | bytes 2883584 | tf_op jit(solution)/shard_map/dot_general | solution.py:65
  15.0 59.5 %all-gather.4.cloned.1.call-done = bf16[1024,1024]{1,0:T(8,128)(2,1)} async-done(((bf16[64,1024]{1,0:T(8,128)(2,1)}), bf16[1024,1024]{1,0:T(8,128)(2,1)}) %all-gather.4.cloned.1.call-update) | async-done | bytes 2097168 | tf_op jit(solution)/shard_map/all_gather | solution.py:32
  74.5 45.9 %while.16 = (s32[]{:T(128)}, f32[1,128,1024]{2,1,0:T(8,128)S(1)}, s32[]{:T(128)}, pred[1,16]{1,0:T(4,128)(4,1)S(1)}, s32[1,16]{1,0:T(1,128)S(1)}, /*index=5*/bf1...) while((s32[]{:T(128)}, f32[1,128,1024]{2,1,0:T(8,128)S(1)}, ...), condition=%wide.region_5.6_spmd, body=%wide.region_2.5_spmd.sunk | while | flops 16908344 | bytes 2261804 | solution.py:62
  75.3 4.7 %conditional.2 = (f32[128,1024]{1,0:T(8,128)S(1)}) conditional(s32[]{:T(128)} %bitcast.26, () %tuple.66, (s32[1,16]{1,0:T(1,128)S(1)}, s32[]{:T(128)}, s32[]{:T(128)}, bf16[1,8,128,128]{3,2,1,0:T(8,128)(2,1)}, s32[]{:T(128)}, /*index=5*/pred[]{:T(512)}, bf16[1024,1024]{1,0:T(8,128)(2,1)}) %tuple.67), branch_computations={%region_3.3_spmd, %region_4.4_spmd} | conditional | flops 16777228 | bytes 688299 | solution.py:58
  78.7 1.2 fusion
  80.8 4.7 %conditional.2 = (f32[128,1024]{1,0:T(8,128)S(1)}) conditional(s32[]{:T(128)} %bitcast.26, () %tuple.66, (s32[1,16]{1,0:T(1,128)S(1)}, s32[]{:T(128)}, s32[]{:T(128)}, bf16[1,8,128,128]{3,2,1,0:T(8,128)(2,1)}, s32[]{:T(128)}, /*index=5*/pred[]{:T(512)}, bf16[1024,1024]{1,0:T(8,128)(2,1)}) %tuple.67), branch_computations={%region_3.3_spmd, %region_4.4_spmd} | conditional | flops 16777228 | bytes 688299 | solution.py:58
  84.3 1.2 fusion
  86.4 0.8 conditional.2
  88.0 0.8 conditional.2
  89.7 0.8 conditional.2
  91.3 4.7 %conditional.2 = (f32[128,1024]{1,0:T(8,128)S(1)}) conditional(s32[]{:T(128)} %bitcast.26, () %tuple.66, (s32[1,16]{1,0:T(1,128)S(1)}, s32[]{:T(128)}, s32[]{:T(128)}, bf16[1,8,128,128]{3,2,1,0:T(8,128)(2,1)}, s32[]{:T(128)}, /*index=5*/pred[]{:T(512)}, bf16[1024,1024]{1,0:T(8,128)(2,1)}) %tuple.67), branch_computations={%region_3.3_spmd, %region_4.4_spmd} | conditional | flops 16777228 | bytes 688299 | solution.py:58
  94.8 1.2 fusion
  96.9 4.7 %conditional.2 = (f32[128,1024]{1,0:T(8,128)S(1)}) conditional(s32[]{:T(128)} %bitcast.26, () %tuple.66, (s32[1,16]{1,0:T(1,128)S(1)}, s32[]{:T(128)}, s32[]{:T(128)}, bf16[1,8,128,128]{3,2,1,0:T(8,128)(2,1)}, s32[]{:T(128)}, /*index=5*/pred[]{:T(512)}, bf16[1024,1024]{1,0:T(8,128)(2,1)}) %tuple.67), branch_computations={%region_3.3_spmd, %region_4.4_spmd} | conditional | flops 16777228 | bytes 688299 | solution.py:58
  100.3 1.2 fusion
  107.3 4.7 %conditional.2 = (f32[128,1024]{1,0:T(8,128)S(1)}) conditional(s32[]{:T(128)} %bitcast.26, () %tuple.66, (s32[1,16]{1,0:T(1,128)S(1)}, s32[]{:T(128)}, s32[]{:T(128)}, bf16[1,8,128,128]{3,2,1,0:T(8,128)(2,1)}, s32[]{:T(128)}, /*index=5*/pred[]{:T(512)}, bf16[1024,1024]{1,0:T(8,128)(2,1)}) %tuple.67), branch_computations={%region_3.3_spmd, %region_4.4_spmd} | conditional | flops 16777228 | bytes 688299 | solution.py:58
  110.8 1.2 fusion
  112.9 0.8 conditional.2
  120.4 4.8 %all-reduce.1 = bf16[128,1024]{1,0:T(8,128)(2,1)S(1)} all-reduce(f32[128,1024]{1,0:T(8,128)S(1)} %bitcast.28), channel_id=1, replica_groups=mesh['rows'=16,'rep'=2] {'rep'}, use_global_device_ids=true, to_apply=%region_6.7 | all-reduce | flops 131072 | bytes 786432 | tf_op jit(solution)/shard_map/psum | solution.py:63
  125.2 2.6 %fusion.12 = (bf16[128,1024]{1,0:T(8,128)(2,1)}, f32[128,1024]{1,0:T(8,128)S(1)}) fusion(f32[128,1024]{1,0:T(8,128)} %fusion.13, bf16[128,1024]{1,0:T(8,128)(2,1)S(1)} %all-reduce.1, bf16[1024,1024]{1,0:T(8,128)(2,1)S(1)} %copy-done), kind=kOutput, calls=%fused_computation.21 | convolution fusion | flops 268697600 | bytes 3670016 | tf_op jit(solution)/shard_map/dot_general | solution.py:66
  127.8 0.9 fusion.7
  128.8 64.2 %all-gather.6.cloned.1.call-done = f32[256,1024]{1,0:T(8,128)} async-done(((f32[16,1024]{1,0:T(8,128)}), f32[256,1024]{1,0:T(8,128)}) %all-gather.6.cloned.1.call-update) | async-done | bytes 1048592 | tf_op jit(solution)/shard_map/all_gather | solution.py:71
  193.0 1.9 reduce_sum.9
  (66 shorter events, 22.8 us)
Async XLA Ops:
  7.2 118.1 %copy-start = (bf16[1024,1024]{1,0:T(8,128)(2,1)S(1)}, bf16[1024,1024]{1,0:T(8,128)(2,1)}, u32[]{:S(2)}) copy-start(bf16[1024,1024]{1,0:T(8,128)(2,1)} %param.13) | copy-start | bytes 6291460
  7.2 67.3 %all-gather.4.cloned.1.call-start = ((), (), s32[]{:S(2)}) async-start(), calls=%async_computation | async-start | bytes 2228224 | tf_op jit(solution)/shard_map/all_gather | solution.py:32
  9.0 184.0 %all-gather.6.cloned.1.call-start = ((), (), s32[]{:S(2)}) async-start(), calls=%async_computation.1 | async-start | bytes 1114112 | tf_op jit(solution)/shard_map/all_gather | solution.py:71
  120.4 7.4 %copy-start.1 = (s32[128]{0:T(128)S(1)}, s32[128]{0:T(128)}, u32[]{:S(2)}) copy-start(s32[128]{0:T(128)} %param.17) | copy-start | bytes 1540
Sparse Core Ops, SparseCore 0:
  11.3 63.0 all-gather.3
  128.9 64.0 all-gather.5
